TPU v7x, 32 devices: a whole 2x2x4 slice. The times are simulated.
32 devices in a mesh: dp: 16 (over z, x, core), tensor: 2 (over y).
Axes of the slice: x: 2, y: 2, z: 4, core: 2. Of those that a mesh axis runs over, the one named last changes fastest.
Arguments:
- tokens: bfloat16 [16384, 1024], P(('dp', 'tensor')), may hold values from -6 to 6
- cotangent: bfloat16 [16384, 1024], P(('dp', 'tensor')), may hold values from -6 to 6
- starts: int32 [16384], P('dp'), may hold values from 0 to 1023, as said below
- first_gain: bfloat16 [1024], P('dp'), may hold values from 0.5 to 1.5
- first_shift: bfloat16 [1024], P('dp'), may hold values from -3 to 3
- attention: bfloat16 [3, 1024, 1024], P(None, 'dp', 'tensor'), may hold values from -0.1875 to 0.1875
- attention_bias: bfloat16 [2, 16, 64], P(None, 'tensor', 'dp'), may hold values from -2 to 2
- combine: bfloat16 [1024, 1024], P('tensor', 'dp'), may hold values from -1.5 to 1.5
- combine_bias: bfloat16 [1024], P('dp'), may hold values from -3 to 3
- second_gain: bfloat16 [1024], P('dp'), may hold values from 0.5 to 1.5
- second_shift: bfloat16 [1024], P('dp'), may hold values from -3 to 3
- expand: bfloat16 [1024, 4096], P('dp', 'tensor'), may hold values from -0.1875 to 0.1875
- expand_bias: bfloat16 [16, 256], P('tensor', 'dp'), may hold values from -3 to 3
- contract: bfloat16 [4096, 1024], P('tensor', 'dp'), may hold values from -0.09375 to 0.09375
- contract_bias: bfloat16 [1024], P('dp'), may hold values from -4 to 4
Outputs:
- result: float32 [16384, 1024], P(('dp', 'tensor'))
- tokens_grad: float32 [16384, 1024], P(('dp', 'tensor'))
- firstgain_grad: float32 [1024], P(('dp', 'tensor'))
- firstshift_grad: float32 [1024], P(('dp', 'tensor'))
- attention_grad: float32 [3, 1024, 1024], P(None, 'dp', 'tensor')
- attenbias_grad: float32 [2, 16, 64], P(None, 'tensor', 'dp')
- combine_grad: float32 [1024, 1024], P('tensor', 'dp')
- combias_grad: float32 [1024], P(('dp', 'tensor'))
- secondgain_grad: float32 [1024], P(('dp', 'tensor'))
- secondshift_grad: float32 [1024], P(('dp', 'tensor'))
- expand_grad: float32 [1024, 4096], P('dp', 'tensor')
- expbias_grad: float32 [16, 256], P('tensor', 'dp')
- contract_grad: float32 [4096, 1024], P('tensor', 'dp')
- conbias_grad: float32 [1024], P(('dp', 'tensor'))
Inputs may be any that keep to these rules, and one draw needn't show every extreme that they name: Each group's 1024 tokens form consecutive sequences, so no sequence crosses a group's border, and at the first token of each sequence starts equals that token's own position within its group. In every draw some group holds one sequence of all 1024 tokens, and some other group ends with a sequence of one token.
All inputs are finite; a program needn't handle non-finite values.
Results may differ from a plain program's by a relative error of at most 0.02.
Values may be sent and summed in bfloat16 or wider, within the bound.
A program may use at most 256 MiB of HBM per device.

v0:
```python
import math

import jax
import jax.numpy as jnp
from jax import lax
from jax.sharding import PartitionSpec as P

H = 16
HD = 64
FF = 4096


EPSILON = 1e-05
SQRT_TWO_PI = 0.7978845608028654
CUBIC = 0.044715
BLOCK_ROWS = 512


def normalize(values):
    center = values - jnp.mean(values, axis=-1, keepdims=True)
    inverse = lax.rsqrt(jnp.mean(center * center, axis=-1, keepdims=True) + EPSILON)
    return (center * inverse, inverse)


def normalize_back(upstream, unit_rows, inverse, gain):
    scaled = upstream * gain
    return inverse * (
        scaled
        - jnp.mean(scaled, axis=-1, keepdims=True)
        - unit_rows * jnp.mean(scaled * unit_rows, axis=-1, keepdims=True)
    )


def gelu_tanh(hidden):
    return (
        0.5 * hidden * (1.0 + jnp.tanh(SQRT_TWO_PI * (hidden + CUBIC * hidden * hidden * hidden)))
    )


def visible(starts, offset, rows_block):
    row_index = offset + jnp.arange(rows_block, dtype=jnp.int32)
    col_index = jnp.arange(starts.shape[0], dtype=jnp.int32)
    row_start = starts[offset : offset + rows_block]
    return (col_index[None, :] >= row_start[:, None]) & (col_index[None, :] <= row_index[:, None])


def block_scores(queries3, keys3, starts, offset, rows_block, scaling):
    scores = (
        jnp.einsum(
            "qhd,khd->hqk",
            queries3[offset : offset + rows_block],
            keys3,
            preferred_element_type=jnp.float32,
        )
        * scaling
    )
    return jnp.where(visible(starts, offset, rows_block)[None], scores, -jnp.inf)


def attend_forward(queries, key_rows, value_rows, starts):
    length = queries.shape[0]
    heads_here = queries.shape[1] // HD
    scaling = 1.0 / math.sqrt(HD)
    queries3 = queries.reshape(length, heads_here, HD)
    keys3 = key_rows.reshape(length, heads_here, HD)
    values3 = value_rows.reshape(length, heads_here, HD)
    rows_block = min(BLOCK_ROWS, length)
    contexts = []
    logsums = []
    for offset in range(0, length, rows_block):
        scores = block_scores(queries3, keys3, starts, offset, rows_block, scaling)
        row_peak = jnp.max(scores, axis=-1, keepdims=True)
        logsum = row_peak + jnp.log(jnp.sum(jnp.exp(scores - row_peak), axis=-1, keepdims=True))
        weights = jnp.exp(scores - logsum).astype(jnp.bfloat16)
        context = jnp.einsum("hqk,khd->qhd", weights, values3, preferred_element_type=jnp.float32)
        contexts.append(context.astype(jnp.bfloat16).reshape(rows_block, heads_here * HD))
        logsums.append(logsum)
    return (jnp.concatenate(contexts, axis=0), jnp.concatenate(logsums, axis=1))


def attend_backward(queries, key_rows, value_rows, context, grad_context, logsums, starts):
    length = queries.shape[0]
    heads_here = queries.shape[1] // HD
    scaling = 1.0 / math.sqrt(HD)
    queries3 = queries.reshape(length, heads_here, HD)
    keys3 = key_rows.reshape(length, heads_here, HD)
    values3 = value_rows.reshape(length, heads_here, HD)
    context3 = context.reshape(length, heads_here, HD)
    grad3 = grad_context.reshape(length, heads_here, HD)
    rows_block = min(BLOCK_ROWS, length)
    grad_keys = jnp.zeros((length, heads_here, HD), jnp.float32)
    grad_values = jnp.zeros((length, heads_here, HD), jnp.float32)
    grad_blocks = []
    for offset in range(0, length, rows_block):
        scores = block_scores(queries3, keys3, starts, offset, rows_block, scaling)
        probability = jnp.exp(scores - logsums[:, offset : offset + rows_block])
        prob_half = probability.astype(jnp.bfloat16)
        grad_here = grad3[offset : offset + rows_block]
        grad_prob = jnp.einsum(
            "qhd,khd->hqk", grad_here, values3, preferred_element_type=jnp.float32
        )
        correction = jnp.einsum(
            "qhd,qhd->hq",
            grad_here.astype(jnp.float32),
            context3[offset : offset + rows_block].astype(jnp.float32),
        )
        grad_scores = (probability * (grad_prob - correction[..., None]) * scaling).astype(
            jnp.bfloat16
        )
        grad_blocks.append(
            jnp.einsum("hqk,khd->qhd", grad_scores, keys3, preferred_element_type=jnp.float32)
        )
        grad_keys = grad_keys + jnp.einsum(
            "hqk,qhd->khd",
            grad_scores,
            queries3[offset : offset + rows_block],
            preferred_element_type=jnp.float32,
        )
        grad_values = grad_values + jnp.einsum(
            "hqk,qhd->khd", prob_half, grad_here, preferred_element_type=jnp.float32
        )
    grad_queries = jnp.concatenate(grad_blocks, axis=0).reshape(length, heads_here * HD)
    return (
        grad_queries,
        grad_keys.reshape(length, heads_here * HD),
        grad_values.reshape(length, heads_here * HD),
    )


def unpack(fetched):
    attend_w, combine_w, expand_w, contract_w, attbias, expbias = fetched[:6]
    vectors = tuple((member.astype(jnp.float32) for member in fetched[6:]))
    heads_bias = attbias.astype(jnp.float32).reshape(2, -1)
    return (
        attend_w,
        combine_w,
        expand_w,
        contract_w,
        heads_bias[0],
        heads_bias[1],
        expbias.astype(jnp.float32).reshape(-1),
    ) + vectors


def gather_rows(normed):
    return lax.all_gather(normed, "tensor", axis=0, tiled=True)


def gather_again(normed):
    return lax.all_gather(normed, "tensor", axis=0, tiled=True)


def gather_grads(gradient):
    return lax.all_gather(gradient, "tensor", axis=0, tiled=True)


def reduce_rows(partial_sum):
    return lax.psum_scatter(
        partial_sum.astype(jnp.bfloat16), "tensor", scatter_dimension=0, tiled=True
    ).astype(jnp.float32)


def sum_inputs(partial_sum):
    return lax.psum_scatter(
        partial_sum.astype(jnp.bfloat16), "tensor", scatter_dimension=0, tiled=True
    ).astype(jnp.float32)


def local(
    tokens,
    cotangent,
    starts,
    first_gain,
    first_shift,
    attention,
    attention_bias,
    combine,
    combine_bias,
    second_gain,
    second_shift,
    expand,
    expand_bias,
    contract,
    contract_bias,
):
    fetched = (
        lax.all_gather(attention, "dp", axis=1, tiled=True),
        lax.all_gather(combine, "dp", axis=1, tiled=True),
        lax.all_gather(expand, "dp", axis=0, tiled=True),
        lax.all_gather(contract, "dp", axis=1, tiled=True),
        lax.all_gather(attention_bias, "dp", axis=2, tiled=True),
        lax.all_gather(expand_bias, "dp", axis=1, tiled=True),
        lax.all_gather(first_gain, "dp", axis=0, tiled=True),
        lax.all_gather(first_shift, "dp", axis=0, tiled=True),
        lax.all_gather(combine_bias, "dp", axis=0, tiled=True),
        lax.all_gather(second_gain, "dp", axis=0, tiled=True),
        lax.all_gather(second_shift, "dp", axis=0, tiled=True),
        lax.all_gather(contract_bias, "dp", axis=0, tiled=True),
    )
    (
        full_attention,
        full_combine,
        full_expand,
        full_contract,
        query_bias,
        value_bias,
        hidden_bias,
        gain_one,
        shift_one,
        bias_combine,
        gain_two,
        shift_two,
        bias_contract,
    ) = unpack(fetched)
    tokens_wide = tokens.astype(jnp.float32)
    unit_one, inverse_one = normalize(tokens_wide)
    normed_one = (unit_one * gain_one + shift_one).astype(jnp.bfloat16)
    rows_one = gather_rows(normed_one)
    projected = jnp.einsum(
        "td,pdc->ptc", rows_one, full_attention, preferred_element_type=jnp.float32
    )
    queries = (projected[0] + query_bias).astype(jnp.bfloat16)
    key_rows = projected[1].astype(jnp.bfloat16)
    value_rows = (projected[2] + value_bias).astype(jnp.bfloat16)
    context, logsums = attend_forward(queries, key_rows, value_rows, starts)
    attended = reduce_rows(jnp.dot(context, full_combine, preferred_element_type=jnp.float32))
    residual = tokens_wide + (attended + bias_combine)
    unit_two, inverse_two = normalize(residual)
    normed_two = (unit_two * gain_two + shift_two).astype(jnp.bfloat16)
    rows_two = gather_rows(normed_two)
    hidden = jnp.dot(rows_two, full_expand, preferred_element_type=jnp.float32) + hidden_bias
    activated, gelu_pull = jax.vjp(gelu_tanh, hidden)
    activated = activated.astype(jnp.bfloat16)
    mixed = (
        reduce_rows(jnp.dot(activated, full_contract, preferred_element_type=jnp.float32))
        + bias_contract
    )
    result = residual + mixed
    fetched = (
        lax.all_gather(attention, "dp", axis=1, tiled=True),
        lax.all_gather(combine, "dp", axis=1, tiled=True),
        lax.all_gather(expand, "dp", axis=0, tiled=True),
        lax.all_gather(contract, "dp", axis=1, tiled=True),
        lax.all_gather(attention_bias, "dp", axis=2, tiled=True),
        lax.all_gather(expand_bias, "dp", axis=1, tiled=True),
        lax.all_gather(first_gain, "dp", axis=0, tiled=True),
        lax.all_gather(first_shift, "dp", axis=0, tiled=True),
        lax.all_gather(combine_bias, "dp", axis=0, tiled=True),
        lax.all_gather(second_gain, "dp", axis=0, tiled=True),
        lax.all_gather(second_shift, "dp", axis=0, tiled=True),
        lax.all_gather(contract_bias, "dp", axis=0, tiled=True),
    )
    (
        full_attention,
        full_combine,
        full_expand,
        full_contract,
        query_bias,
        value_bias,
        hidden_bias,
        gain_one,
        shift_one,
        bias_combine,
        gain_two,
        shift_two,
        bias_contract,
    ) = unpack(fetched)
    grad_out_rows = gather_grads(cotangent)
    contract_grad = jnp.einsum(
        "tf,td->fd", activated, grad_out_rows, preferred_element_type=jnp.float32
    )
    grad_hidden = gelu_pull(
        jnp.einsum("td,fd->tf", grad_out_rows, full_contract, preferred_element_type=jnp.float32)
    )[0]
    expbias_grad = jnp.sum(grad_hidden, axis=0).reshape(-1, FF // H)
    grad_hidden_half = grad_hidden.astype(jnp.bfloat16)
    rows_two = gather_again(normed_two)
    expand_grad = jnp.einsum(
        "td,tf->df", rows_two, grad_hidden_half, preferred_element_type=jnp.float32
    )
    grad_normed_two = sum_inputs(
        jnp.einsum("tf,df->td", grad_hidden_half, full_expand, preferred_element_type=jnp.float32)
    )
    cot_wide = cotangent.astype(jnp.float32)
    grad_residual = cot_wide + normalize_back(grad_normed_two, unit_two, inverse_two, gain_two)
    grad_res_rows = gather_grads(grad_residual.astype(jnp.bfloat16))
    combine_grad = jnp.einsum(
        "tc,td->cd", context, grad_res_rows, preferred_element_type=jnp.float32
    )
    grad_context = jnp.einsum(
        "td,cd->tc", grad_res_rows, full_combine, preferred_element_type=jnp.float32
    ).astype(jnp.bfloat16)
    grad_queries, grad_keys, grad_values = attend_backward(
        queries, key_rows, value_rows, context, grad_context, logsums, starts
    )
    attbias_grad = jnp.stack([jnp.sum(grad_queries, axis=0), jnp.sum(grad_values, axis=0)]).reshape(
        2, -1, HD
    )
    grad_parts = jnp.stack([grad_queries, grad_keys, grad_values]).astype(jnp.bfloat16)
    rows_one = gather_again(normed_one)
    attention_grad = jnp.einsum(
        "td,ptc->pdc", rows_one, grad_parts, preferred_element_type=jnp.float32
    )
    grad_normed_one = sum_inputs(
        jnp.einsum("ptc,pdc->td", grad_parts, full_attention, preferred_element_type=jnp.float32)
    )
    tokens_grad = grad_residual + normalize_back(grad_normed_one, unit_one, inverse_one, gain_one)
    vector_terms = jnp.stack(
        [
            jnp.sum(grad_normed_one * unit_one, axis=0),
            jnp.sum(grad_normed_one, axis=0),
            jnp.sum(grad_residual, axis=0),
            jnp.sum(grad_normed_two * unit_two, axis=0),
            jnp.sum(grad_normed_two, axis=0),
            jnp.sum(cot_wide, axis=0),
        ]
    )
    spread = lax.psum_scatter(vector_terms, ("dp", "tensor"), scatter_dimension=1, tiled=True)
    summed = (
        lax.psum_scatter(
            attention_grad.astype(jnp.bfloat16), "dp", scatter_dimension=1, tiled=True
        ).astype(jnp.float32),
        lax.psum_scatter(
            combine_grad.astype(jnp.bfloat16), "dp", scatter_dimension=1, tiled=True
        ).astype(jnp.float32),
        lax.psum_scatter(
            attbias_grad.astype(jnp.bfloat16), "dp", scatter_dimension=2, tiled=True
        ).astype(jnp.float32),
        lax.psum_scatter(
            contract_grad.astype(jnp.bfloat16), "dp", scatter_dimension=1, tiled=True
        ).astype(jnp.float32),
        lax.psum_scatter(
            expand_grad.astype(jnp.bfloat16), "dp", scatter_dimension=0, tiled=True
        ).astype(jnp.float32),
        lax.psum_scatter(
            expbias_grad.astype(jnp.bfloat16), "dp", scatter_dimension=1, tiled=True
        ).astype(jnp.float32),
    )
    return (
        result,
        tokens_grad,
        spread[0],
        spread[1],
        summed[0],
        summed[2],
        summed[1],
        spread[2],
        spread[3],
        spread[4],
        summed[4],
        summed[5],
        summed[3],
        spread[5],
    )


def solution(mesh):
    in_specs = (
        P(("dp", "tensor"), None),
        P(("dp", "tensor"), None),
        P("dp"),
        P("dp"),
        P("dp"),
        P(None, "dp", "tensor"),
        P(None, "tensor", "dp"),
        P("tensor", "dp"),
        P("dp"),
        P("dp"),
        P("dp"),
        P("dp", "tensor"),
        P("tensor", "dp"),
        P("tensor", "dp"),
        P("dp"),
    )
    out_specs = (
        P(("dp", "tensor"), None),
        P(("dp", "tensor"), None),
        P(("dp", "tensor")),
        P(("dp", "tensor")),
        P(None, "dp", "tensor"),
        P(None, "tensor", "dp"),
        P("tensor", "dp"),
        P(("dp", "tensor")),
        P(("dp", "tensor")),
        P(("dp", "tensor")),
        P("dp", "tensor"),
        P("tensor", "dp"),
        P("tensor", "dp"),
        P(("dp", "tensor")),
    )
    return jax.shard_map(local, mesh=mesh, in_specs=in_specs, out_specs=out_specs, check_vma=False)
```

profile of v0, /device:TPU:0, one launch (start us, length us, event | category | flops | bytes accessed | tf_op | source)
XLA Modules:
  0.0 1105.3 jit_solution(3720705945008971359)
XLA Ops:
  16.6 63.0 %all-reduce.9 = (bf16[1024]{0:T(1024)(128)(2,1)S(1)}, bf16[1024]{0:T(1024)(128)(2,1)S(1)}, bf16[1024]{0:T(1024)(128)(2,1)S(1)}, bf16[1024]{0:T(1024)(128)(2,1)S(1)}, bf16[1024]{0:T(1024)(128)(2,1)S(1)}) all-reduce(bf16[1024]{0:T(1024)(128)(2,1)S(1)} %dynamic-update-slice.4, ...), channel_id=1, replica_groups=mesh['dp'=16,'tensor'=2] {'dp'}, use_global_device_ids=true, to_apply=%add.4 | all-reduce | flops 5120 | bytes 20480
  83.8 17.4 %all_gather.60 = bf16[2,8,64]{1,0,2:T(2,128)(2,1)S(1)} all-gather(bf16[2,8,4]{1,0,2:T(2,128)(2,1)S(1)} %copy.43), channel_id=1, replica_groups=mesh['dp'=16,'tensor'=2] {'dp'}, dimensions={2}, use_global_device_ids=true | all-gather | bytes 2176 | tf_op jit(solution)/shard_map/all_gather | solution.py:191
  102.8 9.9 all-gather.10.cloned.1.call-done
  112.7 47.7 %all-gather.12.cloned.1.call-done = bf16[3,1024,512]{2,1,0:T(8,128)(2,1)} async-done(((bf16[3,64,512]{2,1,0:T(8,128)(2,1)}), bf16[3,1024,512]{2,1,0:T(8,128)(2,1)}) %all-gather.12.cloned.1.call-update) | async-done | bytes 3145744 | tf_op jit(solution)/shard_map/all_gather | solution.py:187
  183.9 8.3 exponential_reduce_fusion
  197.4 8.0 convolution_convert_fusion.6
  210.2 29.7 %reduce-scatter.15.cloned.1.call-done = bf16[512,1024]{1,0:T(8,128)(2,1)} async-done(((bf16[1024,1024]{1,0:T(8,128)(2,1)}), bf16[512,1024]{1,0:T(8,128)(2,1)}) %reduce-scatter.15.cloned.1.call-update) | async-done | bytes 1048592 | tf_op jit(solution)/shard_map/reduce_scatter | solution.py:158
  246.6 21.7 %all-gather = bf16[16,16,8]{1,2,0:T(8,128)(2,1)S(1)} all-gather(bf16[1,16,8]{1,2,0:T(8,128)(2,1)S(1)} %bitcast.161), channel_id=1, replica_groups=mesh['dp'=16,'tensor'=2] {'dp'}, dimensions={0}, use_global_device_ids=true | all-gather | bytes 4352 | tf_op jit(solution)/shard_map/all_gather | solution.py:192
  268.4 24.0 %all-gather.18.cloned.1.call-done = bf16[1024,2048]{1,0:T(8,128)(2,1)} async-done(((bf16[64,2048]{1,0:T(8,128)(2,1)}), bf16[1024,2048]{1,0:T(8,128)(2,1)}) %all-gather.18.cloned.1.call-update) | async-done | bytes 4194320 | tf_op jit(solution)/shard_map/all_gather | solution.py:189
  292.4 33.6 %all-gather.16.cloned.1.call-done = bf16[1024,1024]{1,0:T(8,128)(2,1)} async-done(((bf16[512,1024]{1,0:T(8,128)(2,1)}), bf16[1024,1024]{1,0:T(8,128)(2,1)}) %all-gather.16.cloned.1.call-update) | async-done | bytes 2097168 | tf_op jit(solution)/shard_map/all_gather | solution.py:146
  326.0 10.9 fusion.66
  336.9 23.8 %all-gather.22.cloned.1.call-done = bf16[1024,1024]{1,0:T(8,128)(2,1)} async-done(((bf16[512,1024]{1,0:T(8,128)(2,1)}), bf16[1024,1024]{1,0:T(8,128)(2,1)}) %all-gather.22.cloned.1.call-update) | async-done | bytes 2097168 | tf_op jit(solution)/shard_map/all_gather | solution.py:154
  360.7 52.6 %all-gather.20.cloned.1.call-done = bf16[2048,1024]{0,1:T(8,128)(2,1)} async-done(((bf16[2048,64]{0,1:T(8,128)(2,1)}), bf16[2048,1024]{0,1:T(8,128)(2,1)}) %all-gather.20.cloned.1.call-update) | async-done | bytes 4194320 | tf_op jit(solution)/shard_map/all_gather | solution.py:190
  413.3 14.9 %fusion.56 = (bf16[2048]{0:T(1024)(128)(2,1)S(1)}, bf16[1024,2048]{1,0:T(8,128)(2,1)S(1)}) fusion(f32[1024,2048]{1,0:T(8,128)} %fusion.66, f32[2048]{0:T(1024)S(1)} %bitcast.157, bf16[1024,1024]{1,0:T(8,128)(2,1)} %all-gather.22.cloned.1.call-done, bf16[2048,1024]{0,1:T(8,128)(2,1)} %all-gather.20.cloned.1.call-done), kind=kOutput, calls=%fused_computation.123 | convolution fusion | flops 4349491200 | bytes 18886656 | tf_op jit(solution)/shard_map/td,fd->tf/dot_general | solution.py:273
  435.9 30.6 %reduce-scatter.19.cloned.1.call-done = bf16[512,1024]{1,0:T(8,128)(2,1)} async-done(((bf16[1024,1024]{1,0:T(8,128)(2,1)}), bf16[512,1024]{1,0:T(8,128)(2,1)}) %reduce-scatter.19.cloned.1.call-update) | async-done | bytes 1048592 | tf_op jit(solution)/shard_map/reduce_scatter | solution.py:164
  475.5 10.3 convolution_convert_fusion
  487.4 8.3 convolution_convert_fusion.1
  495.8 11.9 %all-gather.24.cloned.1.call-done = bf16[1024,1024]{1,0:T(8,128)(2,1)} async-done(((bf16[512,1024]{1,0:T(8,128)(2,1)}), bf16[1024,1024]{1,0:T(8,128)(2,1)}) %all-gather.24.cloned.1.call-update) | async-done | bytes 2097168 | tf_op jit(solution)/shard_map/all_gather | solution.py:154
  512.7 12.6 %multiply_convert_fusion.1 = bf16[8,512,1024]{2,1,0:T(8,128)(2,1)} fusion(f32[8,512,1024]{2,1,0:T(8,128)} %copy-done.1, bf16[512,8,64]{0,2,1:T(8,128)(2,1)} %bitcast.145, bf16[1024,8,64]{0,2,1:T(8,128)(2,1)} %copy-done.17, f32[8,512]{1,0:T(8,128)} %get-tuple-element.86, f32[8,512]{1,0:T(8,128)} %copy-done.35, pred[512,1024]{1,0:T(8,128)(4,1)} %copy-done.13), kind=kOutput, calls=%fused_computation.1 | convolution fusion | flops 566231040 | bytes 27295744 | tf_op jit(solution)/shard_map/qhd,khd->hqk/dot_general | solution.py:99
  525.3 7.8 fusion.59
  533.2 10.3 multiply_convert_fusion
  563.4 8.1 fusion.53
  571.6 10.9 bitcast_convert_fusion.1
  592.0 7.6 copy.51
  611.4 11.3 %convolution_convert_fusion.2 = bf16[1024,1024]{1,0:T(8,128)(2,1)} fusion(bf16[2048,1024]{0,1:T(8,128)(2,1)} %all-gather.20.cloned.1.call-done, f32[1024,2048]{1,0:T(8,128)} %fusion.66, f32[2048]{0:T(1024)S(1)} %bitcast.159), kind=kOutput, calls=%fused_computation.85 | convolution fusion | flops 4316987392 | bytes 14688256 | tf_op jit(solution)/shard_map/dot_general | solution.py:235
  627.7 61.8 %all-reduce.8 = (bf16[1024]{0:T(1024)(128)(2,1)S(1)}, bf16[2,8,64]{1,2,0:T(8,128)(2,1)S(1)}) all-reduce(bf16[1024]{0:T(1024)(128)(2,1)S(1)} %dynamic-update-slice.5, bf16[2,8,64]{1,2,0:T(8,128)(2,1)S(1)} %copy.52), channel_id=1, replica_groups=mesh['dp'=16,'tensor'=2] {'dp'}, use_global_device_ids=true, to_apply=%add.5 | all-reduce | flops 2048 | bytes 8192
  691.9 23.0 %reduce-scatter.25.cloned.1.call-done = bf16[64,2048]{1,0:T(8,128)(2,1)} async-done(((bf16[1024,2048]{1,0:T(8,128)(2,1)}), bf16[64,2048]{1,0:T(8,128)(2,1)}) %reduce-scatter.25.cloned.1.call-update) | async-done | bytes 262160 | tf_op jit(solution)/shard_map/reduce_scatter | solution.py:332
  716.7 111.8 %all-reduce.12.cloned.1.call-done = bf16[3,1024,512]{2,0,1:T(4,128)(2,1)} async-done(((bf16[3,1024,512]{2,0,1:T(4,128)(2,1)}), bf16[3,1024,512]{2,0,1:T(4,128)(2,1)}) %all-reduce.12.cloned.1.call-update) | async-done | bytes 3145744
  830.4 58.3 %reduce-scatter.23.cloned.1.call-done = bf16[512,64]{0,1:T(8,128)(2,1)} async-done(((bf16[512,1024]{0,1:T(8,128)(2,1)}), bf16[512,64]{0,1:T(8,128)(2,1)}) %reduce-scatter.23.cloned.1.call-update) | async-done | bytes 65552 | tf_op jit(solution)/shard_map/reduce_scatter | solution.py:323
  890.2 31.6 %reduce-scatter.21.cloned.1.call-done = bf16[512,1024]{1,0:T(8,128)(2,1)} async-done(((bf16[1024,1024]{1,0:T(8,128)(2,1)}), bf16[512,1024]{1,0:T(8,128)(2,1)}) %reduce-scatter.21.cloned.1.call-update) | async-done | bytes 1048592 | tf_op jit(solution)/shard_map/reduce_scatter | solution.py:164
  925.2 30.6 %reduce-scatter.17.cloned.1.call-done = bf16[512,1024]{1,0:T(8,128)(2,1)} async-done(((bf16[1024,1024]{1,0:T(8,128)(2,1)}), bf16[512,1024]{1,0:T(8,128)(2,1)}) %reduce-scatter.17.cloned.1.call-update) | async-done | bytes 1048592 | tf_op jit(solution)/shard_map/reduce_scatter | solution.py:158
  961.0 132.7 %reduce-scatter.29.cloned.1.call-done = f32[32,6]{1,0:T(8,128)} async-done(((f32[1024,6]{1,0:T(8,128)}), f32[32,6]{1,0:T(8,128)}) %reduce-scatter.29.cloned.1.call-update) | async-done | bytes 784
  (247 shorter events, 142.8 us)
Async XLA Ops:
  7.2 76.6 %copy-start.43 = (bf16[2,8,4]{1,2,0:T(4,128)(2,1)S(1)}, bf16[2,8,4]{1,2,0:T(4,128)(2,1)}, u32[]{:S(2)}) copy-start(bf16[2,8,4]{1,2,0:T(4,128)(2,1)} %param.21) | copy-start | bytes 388
  7.2 76.6 %copy-start.41 = (s32[1024]{0:T(1024)S(1)}, s32[1024]{0:T(1024)}, u32[]{:S(2)}) copy-start(s32[1024]{0:T(1024)} %param.17) | copy-start | bytes 12292
  7.2 105.5 %all-gather.10.cloned.1.call-start = ((), (), s32[]{:S(2)}) async-start(), calls=%async_computation.9 | async-start | bytes 3145728 | tf_op jit(solution)/shard_map/all_gather | solution.py:146
  8.7 75.1 %copy-start.28 = (f32[512]{0:T(512)}, f32[512]{0:T(512)S(1)}, u32[]{:S(2)}) copy-start(f32[512]{0:T(512)S(1)} %broadcast_multiply_fusion.5) | copy-start | bytes 6148
  10.4 73.4 %copy-start.30 = (f32[512]{0:T(512)}, f32[512]{0:T(512)S(1)}, u32[]{:S(2)}) copy-start(f32[512]{0:T(512)S(1)} %add_rsqrt_fusion.1) | copy-start | bytes 6148
  82.2 78.3 %all-gather.12.cloned.1.call-start = ((), (), s32[]{:S(2)}) async-start(), calls=%async_computation.10 | async-start | bytes 3342336 | tf_op jit(solution)/shard_map/all_gather | solution.py:187
  83.0 122.5 %all-gather.14.cloned.1.call-start = ((), (), s32[]{:S(2)}) async-start(), calls=%async_computation.11 | async-start | bytes 1114112 | tf_op jit(solution)/shard_map/all_gather | solution.py:188
  83.7 156.2 %reduce-scatter.15.cloned.1.call-start = ((), (), s32[]{:S(2)}) async-start(), calls=%async_computation.12 | async-start | bytes 3145728 | tf_op jit(solution)/shard_map/reduce_scatter | solution.py:158
  102.8 89.6 %copy-start.13 = (pred[512,1024]{1,0:T(8,128)(4,1)}, pred[512,1024]{1,0:T(8,128)(4,1)S(1)}, u32[]{:S(2)}) copy-start(pred[512,1024]{1,0:T(8,128)(4,1)S(1)} %get-tuple-element.110) | copy-start | bytes 1572868
  102.8 94.5 %copy-start.11 = (pred[512,1024]{1,0:T(8,128)(4,1)}, pred[512,1024]{1,0:T(8,128)(4,1)S(1)}, u32[]{:S(2)}) copy-start(pred[512,1024]{1,0:T(8,128)(4,1)S(1)} %get-tuple-element.111) | copy-start | bytes 1572868
  205.5 34.4 %copy-start = (bf16[512,1024]{1,0:T(8,128)(2,1)S(1)}, bf16[512,1024]{1,0:T(8,128)(2,1)}, u32[]{:S(2)}) copy-start(bf16[512,1024]{1,0:T(8,128)(2,1)} %param.15) | copy-start | bytes 3145732
  209.5 82.9 %all-gather.18.cloned.1.call-start = ((), (), s32[]{:S(2)}) async-start(), calls=%async_computation.14 | async-start | bytes 4456448 | tf_op jit(solution)/shard_map/all_gather | solution.py:189
  210.1 115.9 %all-gather.16.cloned.1.call-start = ((), (), s32[]{:S(2)}) async-start(), calls=%async_computation.13 | async-start | bytes 3145728 | tf_op jit(solution)/shard_map/all_gather | solution.py:146
  245.1 115.7 %all-gather.22.cloned.1.call-start = ((), (), s32[]{:S(2)}) async-start(), calls=%async_computation.17 | async-start | bytes 3145728 | tf_op jit(solution)/shard_map/all_gather | solution.py:154
  245.8 167.5 %all-gather.20.cloned.1.call-start = ((), (), s32[]{:S(2)}) async-start(), calls=%async_computation.15 | async-start | bytes 4456448 | tf_op jit(solution)/shard_map/all_gather | solution.py:190
  246.6 219.9 %reduce-scatter.19.cloned.1.call-start = ((), (), s32[]{:S(2)}) async-start(), calls=%async_computation.18 | async-start | bytes 3145728 | tf_op jit(solution)/shard_map/reduce_scatter | solution.py:164
  268.4 207.1 %copy-start.39 = (f32[1,2,8,128]{3,1,2,0:T(2,128)}, f32[1,2,8,128]{3,1,2,0:T(2,128)S(1)}, u32[]{:S(2)}) copy-start(f32[1,2,8,128]{3,1,2,0:T(2,128)S(1)} %copy.81) | copy-start | bytes 24580
  435.9 71.8 %all-gather.24.cloned.1.call-start = ((), (), s32[]{:S(2)}) async-start(), calls=%async_computation.19 | async-start | bytes 3145728 | tf_op jit(solution)/shard_map/all_gather | solution.py:154
  474.4 149.9 %reduce-scatter.31.cloned.1.call-start = ((), (), s32[]{:S(2)}) async-start(), calls=%async_computation.25 | async-start | bytes 69632
  475.3 214.9 %reduce-scatter.27.cloned.1.call-start = ((), (), s32[]{:S(2)}) async-start(), calls=%async_computation.23 | async-start | bytes 4456448 | tf_op jit(solution)/shard_map/reduce_scatter | solution.py:329
  485.8 229.1 %reduce-scatter.25.cloned.1.call-start = ((), (), s32[]{:S(2)}) async-start(), calls=%async_computation.22 | async-start | bytes 4456448 | tf_op jit(solution)/shard_map/reduce_scatter | solution.py:332
  495.7 332.8 %all-reduce.12.cloned.1.call-start = ((), (), s32[]{:S(2)}) async-start(), calls=%async_computation.26 | async-start | bytes 8388608
  599.7 289.0 %reduce-scatter.23.cloned.1.call-start = ((), (), s32[]{:S(2)}) async-start(), calls=%async_computation.21 | async-start | bytes 1114112 | tf_op jit(solution)/shard_map/reduce_scatter | solution.py:323
  604.2 317.6 %reduce-scatter.21.cloned.1.call-start = ((), (), s32[]{:S(2)}) async-start(), calls=%async_computation.20 | async-start | bytes 3145728 | tf_op jit(solution)/shard_map/reduce_scatter | solution.py:164
  611.3 344.4 %reduce-scatter.17.cloned.1.call-start = ((), (), s32[]{:S(2)}) async-start(), calls=%async_computation.16 | async-start | bytes 3145728 | tf_op jit(solution)/shard_map/reduce_scatter | solution.py:158
  622.7 299.1 %copy-start.27 = (f32[1024]{0:T(1024)S(1)}, f32[1024]{0:T(1024)}, u32[]{:S(2)}) copy-start(f32[1024]{0:T(1024)} %copy-done.26) | copy-start | bytes 12292
  622.7 299.1 %copy-start.29 = (f32[512]{0:T(512)S(1)}, f32[512]{0:T(512)}, u32[]{:S(2)}) copy-start(f32[512]{0:T(512)} %copy-done.28) | copy-start | bytes 6148
  622.7 299.1 %copy-start.31 = (f32[512]{0:T(512)S(1)}, f32[512]{0:T(512)}, u32[]{:S(2)}) copy-start(f32[512]{0:T(512)} %copy-done.30) | copy-start | bytes 6148
  622.7 301.3 %copy-start.32 = (f32[1024]{0:T(1024)S(1)}, f32[1024]{0:T(1024)}, u32[]{:S(2)}) copy-start(f32[1024]{0:T(1024)} %get-tuple-element.73) | copy-start | bytes 12292
  622.7 301.3 %copy-start.33 = (f32[1024]{0:T(1024)S(1)}, f32[1024]{0:T(1024)}, u32[]{:S(2)}) copy-start(f32[1024]{0:T(1024)} %get-tuple-element.79) | copy-start | bytes 12292
  622.8 471.0 %reduce-scatter.29.cloned.1.call-start = ((), (), s32[]{:S(2)}) async-start(), calls=%async_computation.24 | async-start | bytes 540672
  625.7 330.1 %copy-start.3 = (bf16[512,1024]{1,0:T(8,128)(2,1)S(1)}, bf16[512,1024]{1,0:T(8,128)(2,1)}, u32[]{:S(2)}) copy-start(bf16[512,1024]{1,0:T(8,128)(2,1)} %reduce-scatter.15.cloned.1.call-done) | copy-start | bytes 3145732
  (41 other events, 397.8 us)
Sparse Core Ops, SparseCore 0:
  82.3 30.3 all-gather.9
  114.9 45.4 all-gather.11
  162.6 36.2 all-gather.13
  209.6 30.2 reduce-scatter.14
  241.9 50.4 all-gather.17
  294.4 31.6 all-gather.15
  327.6 33.0 all-gather.21
  362.9 50.3 all-gather.19
  436.0 30.4 reduce-scatter.18
  474.6 33.0 all-gather.23
  511.6 51.8 reduce-scatter.30
  567.2 71.9 reduce-scatter.26
  643.0 71.8 reduce-scatter.24
  718.4 110.0 all-reduce.11
  832.0 56.6 reduce-scatter.22
  890.8 30.9 reduce-scatter.20
  923.9 31.8 reduce-scatter.16
  957.9 135.7 reduce-scatter.28
where the time goes:
time: 1110 us
  waiting for transfers between devices  655 us (59%)
  matrix products  183 us (16%)
  blocking collectives  164 us (15%)
  other arithmetic  50.3 us (5%)
  local copies, waits for them, and re-layouts  34.7 us (3%)
  between operations  17.4 us (2%)
    unnamed x21, waiting for transfers between devices  248 us
    unnamed x2, blocking collectives  125 us
    reduce_scatter x2, waiting for transfers between devices, sum_inputs(): lax.psum_scatter(partial_sum.astype(jnp.bfloat16), 'tensor', scatter_dime...  62.2 us
    reduce_scatter x2, waiting for transfers between devices, reduce_rows(): lax.psum_scatter(partial_sum.astype(jnp.bfloat16), 'tensor', scatter_dime...  60.3 us
    reduce_scatter x1, waiting for transfers between devices, local(): lax.psum_scatter(combine_grad.astype(jnp.bfloat16), 'dp', scatter_dimensi...  58.3 us
    all_gather x1, waiting for transfers between devices, local(): lax.all_gather(contract, 'dp', axis=1, tiled=True)  52.6 us
    all_gather x1, waiting for transfers between devices, local(): lax.all_gather(attention, 'dp', axis=1, tiled=True)  47.7 us
    all_gather x2, waiting for transfers between devices, gather_rows(): return lax.all_gather(normed, 'tensor', axis=0, tiled=True)  43.5 us
  transfers between devices with their start and end apart: 18, of which 15 were waited for; matrix products, arithmetic and copies ran while one was open for 19% of the time, Pallas kernels for 0%

commit v1 on v0

v1 whole, which is shorter than its diff:
```python
import math

import jax
import jax.numpy as jnp
from jax import lax
from jax.sharding import PartitionSpec as P

H = 16
HD = 64
FF = 4096


EPSILON = 1e-05
SQRT_TWO_PI = 0.7978845608028654
CUBIC = 0.044715
BLOCK_ROWS = 512


def normalize(values):
    center = values - jnp.mean(values, axis=-1, keepdims=True)
    inverse = lax.rsqrt(jnp.mean(center * center, axis=-1, keepdims=True) + EPSILON)
    return (center * inverse, inverse)


def normalize_back(upstream, unit_rows, inverse, gain):
    scaled = upstream * gain
    return inverse * (
        scaled
        - jnp.mean(scaled, axis=-1, keepdims=True)
        - unit_rows * jnp.mean(scaled * unit_rows, axis=-1, keepdims=True)
    )


def gelu_tanh(hidden):
    return (
        0.5 * hidden * (1.0 + jnp.tanh(SQRT_TWO_PI * (hidden + CUBIC * hidden * hidden * hidden)))
    )


def visible(starts, offset, rows_block):
    row_index = offset + jnp.arange(rows_block, dtype=jnp.int32)
    col_index = jnp.arange(starts.shape[0], dtype=jnp.int32)
    row_start = starts[offset : offset + rows_block]
    return (col_index[None, :] >= row_start[:, None]) & (col_index[None, :] <= row_index[:, None])


def block_scores(queries3, keys3, starts, offset, rows_block, scaling):
    span = offset + rows_block
    scores = (
        jnp.einsum(
            "qhd,khd->hqk",
            queries3[offset:span],
            keys3[:span],
            preferred_element_type=jnp.float32,
        )
        * scaling
    )
    seen = visible(starts, offset, rows_block)[:, :span]
    return jnp.where(seen[None], scores, -jnp.inf)


def attend_forward(queries3, keys3, values3, starts, offset, rows_block):
    scaling = 1.0 / math.sqrt(HD)
    span = offset + rows_block
    scores = block_scores(queries3, keys3, starts, offset, rows_block, scaling)
    row_peak = jnp.max(scores, axis=-1, keepdims=True)
    logsum = row_peak + jnp.log(jnp.sum(jnp.exp(scores - row_peak), axis=-1, keepdims=True))
    weights = jnp.exp(scores - logsum).astype(jnp.bfloat16)
    context = jnp.einsum(
        "hqk,khd->qhd", weights, values3[:span], preferred_element_type=jnp.float32
    )
    return context.astype(jnp.bfloat16).reshape(rows_block, -1), logsum


def attend_backward(queries3, keys3, values3, context3, grad3, logsums, starts):
    length = queries3.shape[0]
    scaling = 1.0 / math.sqrt(HD)
    rows_block = min(BLOCK_ROWS, length)
    grad_keys = 0.0
    grad_values = 0.0
    grad_blocks = []
    for place, offset in enumerate(range(0, length, rows_block)):
        span = offset + rows_block
        scores = block_scores(queries3, keys3, starts, offset, rows_block, scaling)
        probability = jnp.exp(scores - logsums[place])
        prob_half = probability.astype(jnp.bfloat16)
        grad_here = grad3[offset:span]
        grad_prob = jnp.einsum(
            "qhd,khd->hqk", grad_here, values3[:span], preferred_element_type=jnp.float32
        )
        correction = jnp.einsum(
            "qhd,qhd->hq",
            grad_here.astype(jnp.float32),
            context3[offset:span].astype(jnp.float32),
        )
        grad_scores = (probability * (grad_prob - correction[..., None]) * scaling).astype(
            jnp.bfloat16
        )
        grad_blocks.append(
            jnp.einsum("hqk,khd->qhd", grad_scores, keys3[:span], preferred_element_type=jnp.float32)
        )
        beyond = ((0, length - span), (0, 0), (0, 0))
        grad_keys = grad_keys + jnp.pad(
            jnp.einsum(
                "hqk,qhd->khd",
                grad_scores,
                queries3[offset:span],
                preferred_element_type=jnp.float32,
            ),
            beyond,
        )
        grad_values = grad_values + jnp.pad(
            jnp.einsum("hqk,qhd->khd", prob_half, grad_here, preferred_element_type=jnp.float32),
            beyond,
        )
    return (
        jnp.concatenate(grad_blocks, axis=0).reshape(length, -1),
        grad_keys.reshape(length, -1),
        grad_values.reshape(length, -1),
    )


SWAP = ((0, 1), (1, 0))


def swap(rows):
    return lax.ppermute(rows, "tensor", SWAP)


def own_rows(rows, count, position):
    return lax.dynamic_slice_in_dim(rows, position * count, count, axis=0)


def gather_rows(rows, parts, position):
    if parts != 2:
        return lax.all_gather(rows, "tensor", axis=0, tiled=True)
    other = swap(rows)
    low = position == 0
    return jnp.concatenate([jnp.where(low, rows, other), jnp.where(low, other, rows)], axis=0)


def sum_full(partial, parts):
    if parts != 2:
        return lax.psum(partial.astype(jnp.bfloat16), "tensor").astype(jnp.float32)
    return partial + swap(partial.astype(jnp.bfloat16)).astype(jnp.float32)


def sum_own(partial, parts, position):
    if parts != 2:
        return lax.psum_scatter(
            partial.astype(jnp.bfloat16), "tensor", scatter_dimension=0, tiled=True
        ).astype(jnp.float32)
    count = partial.shape[0] // 2
    sent = own_rows(partial.astype(jnp.bfloat16), count, 1 - position)
    return own_rows(partial, count, position) + swap(sent).astype(jnp.float32)


def gather_weight(shard):
    return lax.all_gather(shard, "dp", axis=0, tiled=True)


def scatter_grad(grad):
    return lax.psum_scatter(
        grad.astype(jnp.bfloat16), "dp", scatter_dimension=0, tiled=True
    ).astype(jnp.float32)


def as_columns(flat, rows):
    short = -flat.shape[-1] % rows
    flat = jnp.pad(flat, [(0, 0)] * (flat.ndim - 1) + [(0, short)])
    return flat.reshape(-1, (flat.shape[-1]) // rows)


def local(
    tokens,
    cotangent,
    starts,
    first_gain,
    first_shift,
    attention,
    attention_bias,
    combine,
    combine_bias,
    second_gain,
    second_shift,
    expand,
    expand_bias,
    contract,
    contract_bias,
):
    parts = lax.axis_size("tensor")
    position = lax.axis_index("tensor")
    groups = lax.axis_size("dp")
    own_count = tokens.shape[0]
    length = own_count * parts
    shard_rows = first_gain.shape[0]
    columns = attention.shape[2]
    heads_here = columns // HD
    half = jnp.bfloat16

    vectors = jnp.stack(
        [first_gain, first_shift, combine_bias, second_gain, second_shift, contract_bias], axis=1
    )
    bias_flat = jnp.concatenate([attention_bias.reshape(-1), expand_bias.reshape(-1)])
    packed = jnp.concatenate(
        [
            attention.transpose(1, 0, 2).reshape(shard_rows, 3 * columns),
            vectors,
            as_columns(bias_flat, shard_rows),
        ],
        axis=1,
    )
    packed = jnp.pad(packed, ((0, 0), (0, -packed.shape[1] % 128)))
    rows_tokens = gather_rows(tokens, parts, position)
    full_packed = gather_weight(packed)
    full_combine = gather_weight(combine.T)
    full_expand = gather_weight(expand)
    full_contract = gather_weight(contract.T)
    rows_cot = gather_rows(cotangent, parts, position)

    full_attention = full_packed[:, : 3 * columns]
    extra = full_packed[:, 3 * columns :]
    gain_one, shift_one, bias_combine, gain_two, shift_two, bias_contract = (
        extra[:, :6].T.astype(jnp.float32)
    )
    bias_cols = -(-bias_flat.shape[0] // shard_rows)
    bias_rows = extra[:, 6 : 6 + bias_cols].reshape(groups, -1).astype(jnp.float32)
    att_count = attention_bias.size
    heads_bias = (
        bias_rows[:, :att_count]
        .reshape((groups,) + attention_bias.shape)
        .transpose(1, 2, 0, 3)
        .reshape(2, columns)
    )
    hidden_bias = (
        bias_rows[:, att_count : bias_flat.shape[0]]
        .reshape((groups,) + expand_bias.shape)
        .transpose(1, 0, 2)
        .reshape(-1)
    )

    tokens_wide = rows_tokens.astype(jnp.float32)
    unit_one, inverse_one = normalize(tokens_wide)
    rows_one = (unit_one * gain_one + shift_one).astype(half)
    projected = jnp.dot(rows_one, full_attention, preferred_element_type=jnp.float32)
    queries3 = (projected[:, :columns] + heads_bias[0]).astype(half)
    keys3 = projected[:, columns : 2 * columns].astype(half)
    values3 = (projected[:, 2 * columns :] + heads_bias[1]).astype(half)
    queries3, keys3, values3 = (
        member.reshape(length, heads_here, HD) for member in (queries3, keys3, values3)
    )
    rows_block = min(BLOCK_ROWS, length)
    contexts, logsums, attended = [], [], []
    for offset in range(0, length, rows_block):
        context, logsum = attend_forward(queries3, keys3, values3, starts, offset, rows_block)
        contexts.append(context)
        logsums.append(logsum)
        attended.append(
            sum_full(
                jnp.einsum("tc,dc->td", context, full_combine, preferred_element_type=jnp.float32),
                parts,
            )
        )
    context = jnp.concatenate(contexts, axis=0)
    grad_act = jnp.einsum("td,df->tf", rows_cot, full_contract, preferred_element_type=jnp.float32)
    residual = tokens_wide + (jnp.concatenate(attended, axis=0) + bias_combine)
    unit_two, inverse_two = normalize(residual)
    rows_two = (unit_two * gain_two + shift_two).astype(half)
    hidden = jnp.dot(rows_two, full_expand, preferred_element_type=jnp.float32) + hidden_bias
    activated, gelu_pull = jax.vjp(gelu_tanh, hidden)
    activated = activated.astype(half)
    grad_hidden = gelu_pull(grad_act)[0]
    expbias_grad = jnp.sum(grad_hidden, axis=0)
    grad_hidden_half = grad_hidden.astype(half)
    grad_two = []
    for offset in range(0, length, rows_block):
        grad_two.append(
            sum_full(
                jnp.einsum(
                    "tf,df->td",
                    grad_hidden_half[offset : offset + rows_block],
                    full_expand,
                    preferred_element_type=jnp.float32,
                ),
                parts,
            )
        )
    grad_normed_two = jnp.concatenate(grad_two, axis=0)
    contract_grad = scatter_grad(
        jnp.einsum("td,tf->df", rows_cot, activated, preferred_element_type=jnp.float32)
    )
    expand_grad = scatter_grad(
        jnp.einsum("td,tf->df", rows_two, grad_hidden_half, preferred_element_type=jnp.float32)
    )
    mixed = sum_own(
        jnp.einsum("tf,df->td", activated, full_contract, preferred_element_type=jnp.float32),
        parts,
        position,
    )
    result = own_rows(residual, own_count, position) + (mixed + bias_contract)

    cot_wide = rows_cot.astype(jnp.float32)
    grad_residual = cot_wide + normalize_back(grad_normed_two, unit_two, inverse_two, gain_two)
    grad_res_half = grad_residual.astype(half)
    combine_grad = scatter_grad(
        jnp.einsum("td,tc->dc", grad_res_half, context, preferred_element_type=jnp.float32)
    )
    grad_context = jnp.einsum(
        "td,dc->tc", grad_res_half, full_combine, preferred_element_type=jnp.float32
    ).astype(half)
    grad_queries, grad_keys, grad_values = attend_backward(
        queries3,
        keys3,
        values3,
        context.reshape(length, heads_here, HD),
        grad_context.reshape(length, heads_here, HD),
        logsums,
        starts,
    )
    attbias_grad = jnp.stack([jnp.sum(grad_queries, axis=0), jnp.sum(grad_values, axis=0)])
    grad_parts = jnp.concatenate([grad_queries, grad_keys, grad_values], axis=1).astype(half)
    grad_normed_one = sum_own(
        jnp.einsum("tc,dc->td", grad_parts, full_attention, preferred_element_type=jnp.float32),
        parts,
        position,
    )
    attention_grad = jnp.einsum(
        "td,tc->dc", rows_one, grad_parts, preferred_element_type=jnp.float32
    )
    unit_own = own_rows(unit_one, own_count, position)
    tokens_grad = own_rows(grad_residual, own_count, position) + normalize_back(
        grad_normed_one, unit_own, own_rows(inverse_one, own_count, position), gain_one
    )
    vector_grads = jnp.stack(
        [
            jnp.sum(grad_normed_one * unit_own, axis=0),
            jnp.sum(grad_normed_one, axis=0),
            jnp.sum(grad_residual, axis=0),
            jnp.sum(grad_normed_two * unit_two, axis=0),
            jnp.sum(grad_normed_two, axis=0),
            jnp.sum(cot_wide, axis=0),
        ],
        axis=1,
    )
    att_shape = attention_bias.shape
    exp_shape = expand_bias.shape
    bias_grads = jnp.concatenate(
        [
            attbias_grad.reshape(2, heads_here, groups, att_shape[2])
            .transpose(2, 0, 1, 3)
            .reshape(groups, -1),
            expbias_grad.reshape(exp_shape[0], groups, exp_shape[1])
            .transpose(1, 0, 2)
            .reshape(groups, -1),
        ],
        axis=1,
    )
    small_grads = jnp.concatenate([vector_grads, as_columns(bias_grads, shard_rows)], axis=1)
    small_grads = jnp.pad(small_grads, ((0, 0), (0, -small_grads.shape[1] % 128)))
    summed = scatter_grad(jnp.concatenate([attention_grad, small_grads], axis=1))
    attention_grad = summed[:, : 3 * columns].reshape(shard_rows, 3, columns).transpose(1, 0, 2)
    small = summed[:, 3 * columns :]
    paired = small[:, :2]
    paired = paired + swap(paired) if parts == 2 else lax.psum(paired, "tensor")
    spread = jnp.concatenate([paired, small[:, 2:6]], axis=1).T
    share = shard_rows // parts
    spread = lax.dynamic_slice_in_dim(spread, position * share, share, axis=1)
    flat = small[:, 6 : 6 + bias_cols].reshape(-1)
    return (
        result,
        tokens_grad,
        spread[0],
        spread[1],
        attention_grad,
        flat[:att_count].reshape(att_shape),
        combine_grad.T,
        spread[2],
        spread[3],
        spread[4],
        expand_grad,
        flat[att_count : bias_flat.shape[0]].reshape(exp_shape),
        contract_grad.T,
        spread[5],
    )


def solution(mesh):
    in_specs = (
        P(("dp", "tensor"), None),
        P(("dp", "tensor"), None),
        P("dp"),
        P("dp"),
        P("dp"),
        P(None, "dp", "tensor"),
        P(None, "tensor", "dp"),
        P("tensor", "dp"),
        P("dp"),
        P("dp"),
        P("dp"),
        P("dp", "tensor"),
        P("tensor", "dp"),
        P("tensor", "dp"),
        P("dp"),
    )
    out_specs = (
        P(("dp", "tensor"), None),
        P(("dp", "tensor"), None),
        P(("dp", "tensor")),
        P(("dp", "tensor")),
        P(None, "dp", "tensor"),
        P(None, "tensor", "dp"),
        P("tensor", "dp"),
        P(("dp", "tensor")),
        P(("dp", "tensor")),
        P(("dp", "tensor")),
        P("dp", "tensor"),
        P("tensor", "dp"),
        P("tensor", "dp"),
        P(("dp", "tensor")),
    )
    return jax.shard_map(local, mesh=mesh, in_specs=in_specs, out_specs=out_specs, check_vma=False)
```

time: 1110 us -> 585 us (0.53)
  waiting for transfers between devices: 655 us -> 288 us
  blocking collectives: 164 us -> 0 us
  matrix products: 183 us -> 150 us
  local copies, waits for them, and re-layouts: 34.7 us -> 55.6 us
  starting transfers between devices: 1.08 us -> 12.5 us
    unnamed x21 -> x8, waiting for transfers between devices: 248 us -> 1.47 us
    all_gather x8 -> x4, waiting for transfers between devices: 204 us -> 43 us  [gather_weight(): return lax.all_gather(shard, 'dp', axis=0, tiled=True)]
    unnamed x2 -> x0, blocking collectives: 125 us -> none
    ppermute x0 -> x9, waiting for transfers between devices: none -> 123 us  [swap(): return lax.ppermute(rows, 'tensor', SWAP)]
    reduce_scatter x7 -> x4, waiting for transfers between devices: 204 us -> 120 us  [scatter_grad(): lax.psum_scatter(grad.astype(jnp.bfloat16), 'dp', scatter_dimension=0, ti...]
    all_gather x2 -> x0, blocking collectives: 39.1 us -> none  [the longest x1 21.7 us: local(): lax.all_gather(expand_bias, 'dp', axis=1, tiled=True)]
    dot_general x20 -> x22, matrix products: 144 us -> 115 us  [the longest x2 17.2 us: attend_backward(): jnp.einsum('qhd,khd->hqk', grad_here, values3[:span], preferred_element_t...]
    slice x7 -> x24, local copies, waits for them, and re-layouts: 1.35 us -> 20.3 us  [the longest x2 4.02 us: local(): keys3 = projected[:, columns:2 * columns].astype(half)]
  transfers between devices with their start and end apart: 18 -> 17, of which waited for: 15 -> 11; matrix products, arithmetic and copies ran while one was open for 19% -> 37% of each run, Pallas kernels for 0% -> 0%
where the time goes in v1:
time: 585 us; the launch traced here: 577 us
  waiting for transfers between devices  288 us (49%)
  matrix products  150 us (26%)
  other arithmetic  56.2 us (10%)
  local copies, waits for them, and re-layouts  55.6 us (10%)
  between operations  15.4 us (3%)
  starting transfers between devices  12.5 us (2%)
    ppermute x9, waiting for transfers between devices, swap(): return lax.ppermute(rows, 'tensor', SWAP)  123 us
    reduce_scatter x4, waiting for transfers between devices, scatter_grad(): lax.psum_scatter(grad.astype(jnp.bfloat16), 'dp', scatter_dimension=0, ti...  120 us
    all_gather x4, waiting for transfers between devices, gather_weight(): return lax.all_gather(shard, 'dp', axis=0, tiled=True)  43 us
    dot_general x2, matrix products, attend_backward(): jnp.einsum('qhd,khd->hqk', grad_here, values3[:span], preferred_element_t...  17.2 us
    dot_general x1, matrix products, local(): jnp.einsum('td,df->tf', rows_cot, full_contract, preferred_element_type=j...  15.1 us
    dot_general x2, matrix products, attend_backward(): jnp.einsum('hqk,qhd->khd', prob_half, grad_here, preferred_element_type=j...  13.4 us
    dot_general x2, matrix products, attend_forward(): jnp.einsum('hqk,khd->qhd', weights, values3[:span], preferred_element_typ...  11.8 us
    ppermute x9, starting transfers between devices, swap(): return lax.ppermute(rows, 'tensor', SWAP)  11.8 us
  transfers between devices with their start and end apart: 17, of which 11 were waited for; matrix products, arithmetic and copies ran while one was open for 37% of the time, Pallas kernels for 0%

profile of v1, /device:TPU:0, one launch (start us, length us, event | category | flops | bytes accessed | tf_op | source)
XLA Modules:
  0.0 577.5 jit_solution(3608244362095749780)
XLA Ops:
  22.6 21.8 %collective-permute-done = bf16[512,1024]{1,0:T(8,128)(2,1)S(1)} collective-permute-done((bf16[512,1024]{1,0:T(8,128)(2,1)}, bf16[512,1024]{1,0:T(8,128)(2,1)S(1)}, u32[]{:S(2)}, u32[]{:S(2)}) %collective-permute-start) | collective-permute-done | bytes 1048608 | tf_op jit(solution)/shard_map/ppermute | solution.py:127
  46.7 18.2 %all-gather.5.cloned.1.call-done = bf16[1024,1664]{1,0:T(8,128)(2,1)} async-done(((bf16[64,1664]{1,0:T(8,128)(2,1)}), bf16[1024,1664]{1,0:T(8,128)(2,1)}) %all-gather.5.cloned.1.call-update) | async-done | bytes 3407888 | tf_op jit(solution)/shard_map/all_gather | solution.py:159
  69.5 7.1 %fusion.62 = (bf16[1024,1536]{1,0:T(8,128)(2,1)}, f32[1024,1536]{1,0:T(8,128)S(1)}) fusion(bf16[1024,1664]{1,0:T(8,128)(2,1)} %all-gather.5.cloned.1.call-done, f32[1024]{0:T(1024)S(1)} %get-tuple-element.81, f32[1024]{0:T(1024)S(1)} %get-tuple-element.82, f32[1024]{0:T(1024)S(1)} %add_rsqrt_fusion.1, f32[1024]{0:T(1024)S(1)} %broadcast_multiply_fusion.3, ...), kind=kOutput, calls=%fused_computation.160 | convolution fusion | flops 3232235520 | bytes 14696448 | tf_op jit(solution)/shard_map/dot_general | solution.py:245
  84.1 4.2 fusion.1
  88.3 4.3 exponential_reduce_fusion
  100.1 9.5 %convolution_convert_fusion.5 = bf16[8,64,512]{2,1,0:T(8,128)(2,1)} fusion(bf16[1024,8,64]{0,2,1:T(8,128)(2,1)} %bitcast.139, f32[8,512,1024]{2,1,0:T(8,128)} %copy-done.2, f32[8,512]{1,0:T(8,128)S(1)} %log_add_fusion, pred[512,1024]{1,0:T(8,128)(4,1)} %fusion.25), kind=kOutput, calls=%fused_computation.83 | convolution fusion | flops 553910272 | bytes 18890752 | tf_op jit(solution)/shard_map/hqk,khd->qhd/dot_general | solution.py:69
  130.9 4.0 fusion.50
  135.2 4.6 collective-permute-done.2
  142.0 19.5 %collective-permute-done.1 = bf16[512,1024]{1,0:T(8,128)(2,1)} collective-permute-done((bf16[512,1024]{1,0:T(8,128)(2,1)}, bf16[512,1024]{1,0:T(8,128)(2,1)}, u32[]{:S(2)}, u32[]{:S(2)}) %collective-permute-start.1) | collective-permute-done | bytes 1048608 | tf_op jit(solution)/shard_map/ppermute | solution.py:127
  163.1 4.3 fusion.54
  169.9 11.3 %fusion.45 = f32[1024,2048]{1,0:T(8,128)} fusion(bf16[1024,2048]{1,0:T(8,128)(2,1)} %all-gather.9.cloned.1.call-done, f32[1024,1024]{1,0:T(8,128)} %copy-done, f32[1024]{0:T(1024)S(1)} %copy-done.51, f32[1024]{0:T(1024)S(1)} %get-tuple-element.79, f32[1024]{0:T(1024)S(1)} %add_rsqrt_fusion, f32[1024]{0:T(1024)S(1)} %broadcast_multiply_fusion.2), kind=kOutput, calls=%fused_computation.145 | convolution fusion | flops 4300210176 | bytes 16793600 | tf_op jit(solution)/shard_map/dot_general | solution.py:269
  181.2 24.8 %all-gather.11.cloned.1.call-done = bf16[1024,2048]{1,0:T(8,128)(2,1)} async-done(((bf16[64,2048]{1,0:T(8,128)(2,1)}), bf16[1024,2048]{1,0:T(8,128)(2,1)}) %all-gather.11.cloned.1.call-update) | async-done | bytes 4194320 | tf_op jit(solution)/shard_map/all_gather | solution.py:159
  206.0 15.1 %fusion.55 = (bf16[2048]{0:T(1024)(128)(2,1)S(1)}, bf16[1024,2048]{1,0:T(8,128)(2,1)S(1)}) fusion(bf16[1024,2048]{1,0:T(8,128)(2,1)} %all-gather.11.cloned.1.call-done, bf16[512,1024]{1,0:T(8,128)(2,1)} %get-tuple-element.108, bf16[512,1024]{1,0:T(8,128)(2,1)} %get-tuple-element.86, f32[1024,2048]{1,0:T(8,128)} %fusion.45, f32[2048]{0:T(1024)S(1)} %add.216), kind=kOutput, calls=%fused_computation.153 | convolution fusion | flops 4353685504 | bytes 18886656 | tf_op jit(solution)/shard_map/td,df->tf/dot_general | solution.py:265
  228.0 21.6 %collective-permute-done.6 = bf16[512,1024]{1,0:T(8,128)(2,1)S(1)} collective-permute-done((bf16[512,1024]{1,0:T(8,128)(2,1)S(1)}, bf16[512,1024]{1,0:T(8,128)(2,1)S(1)}, u32[]{:S(2)}, u32[]{:S(2)}) %collective-permute-start.6) | collective-permute-done | bytes 1048608 | tf_op jit(solution)/shard_map/ppermute | solution.py:127
  250.1 21.2 %collective-permute-done.5 = bf16[512,1024]{1,0:T(8,128)(2,1)S(1)} collective-permute-done((bf16[512,1024]{1,0:T(8,128)(2,1)S(1)}, bf16[512,1024]{1,0:T(8,128)(2,1)S(1)}, u32[]{:S(2)}, u32[]{:S(2)}) %collective-permute-start.5) | collective-permute-done | bytes 1048608 | tf_op jit(solution)/shard_map/ppermute | solution.py:127
  274.6 4.1 fusion.53
  278.7 4.5 convolution_convert_fusion.3
  283.7 10.4 %convolution_convert_fusion.2 = bf16[1024,2048]{1,0:T(8,128)(2,1)} fusion(bf16[1024,2048]{1,0:T(8,128)(2,1)} %copy-done.54, f32[1024,1024]{1,0:T(8,128)} %copy-done, f32[1024]{0:T(1024)S(1)} %copy-done.51, f32[1024]{0:T(1024)S(1)} %get-tuple-element.79, f32[1024]{0:T(1024)S(1)} %add_rsqrt_fusion, f32[1024]{0:T(1024)S(1)} %broadcast_multiply_fusion.2), kind=kOutput, calls=%fused_computation.41 | convolution fusion | flops 4302307328 | bytes 12599296 | tf_op jit(solution)/shard_map/td,tf->df/dot_general | solution.py:293
  295.9 10.9 %convolution_convert_fusion.1 = bf16[1024,2048]{1,0:T(8,128)(2,1)} fusion(bf16[512,1024]{1,0:T(8,128)(2,1)} %get-tuple-element.108, bf16[512,1024]{1,0:T(8,128)(2,1)} %get-tuple-element.86, f32[1024,2048]{1,0:T(8,128)} %fusion.45, f32[2048]{0:T(1024)S(1)} %copy-done.48), kind=kOutput, calls=%fused_computation.40 | convolution fusion | flops 4322230272 | bytes 14688256 | tf_op jit(solution)/shard_map/td,tf->df/dot_general | solution.py:290
  307.0 4.0 convolution_convert_fusion.4
  311.5 7.3 %multiply_convert_fusion.1 = bf16[8,512,512]{1,2,0:T(8,128)(2,1)} fusion(f32[8,512,512]{1,2,0:T(8,128)} %copy-done.3, f32[8,512]{1,0:T(8,128)S(1)} %get-tuple-element.115, f32[8,512]{1,0:T(8,128)S(1)} %copy-done.44, pred[512,512]{0,1:T(8,128)(4,1)S(1)} %fusion.34, bf16[512,8,64]{0,2,1:T(8,128)(2,1)S(1)} %bitcast.146, bf16[512,8,64]{0,2,1:T(8,128)(2,1)S(1)} %bitcast.149), kind=kOutput, calls=%fused_computation.15 | convolution fusion | flops 283115520 | bytes 13926400 | tf_op jit(solution)/shard_map/qhd,khd->hqk/dot_general | solution.py:88
  318.8 9.9 %multiply_convert_fusion = bf16[8,512,1024]{2,1,0:T(8,128)(2,1)S(1)} fusion(f32[8,512,1024]{2,1,0:T(8,128)} %copy-done.2, bf16[512,8,64]{0,2,1:T(8,128)(2,1)S(1)} %bitcast.144, bf16[1024,8,64]{0,2,1:T(8,128)(2,1)S(1)} %bitcast.140, f32[8,512]{1,0:T(8,128)S(1)} %get-tuple-element.94, f32[8,512]{1,0:T(8,128)S(1)} %copy-done.42, pred[512,1024]{1,0:T(8,128)(4,1)S(1)} %copy-done.10), kind=kOutput, calls=%fused_computation | convolution fusion | flops 566231040 | bytes 27295744 | tf_op jit(solution)/shard_map/qhd,khd->hqk/dot_general | solution.py:88
  336.4 7.2 %convolution_bitcast_fusion = f32[512,8,64]{0,2,1:T(8,128)} fusion(bf16[512,8,64]{0,2,1:T(8,128)(2,1)S(1)} %bitcast.147, f32[8,512,512]{1,2,0:T(8,128)} %copy-done.3, f32[8,512]{1,0:T(8,128)S(1)} %copy-done.44, pred[512,512]{0,1:T(8,128)(4,1)S(1)} %fusion.34), kind=kOutput, calls=%fused_computation.79 | convolution fusion | flops 276824064 | bytes 10240000 | tf_op jit(solution)/shard_map/hqk,qhd->khd/dot_general | solution.py:113
  343.7 6.2 %fusion.56 = (bf16[8,64]{1,0:T(8,128)(2,1)S(1)}, bf16[1024,8,64]{0,2,1:T(8,128)(2,1)S(1)}) fusion(bf16[512,8,64]{0,2,1:T(8,128)(2,1)S(1)} %bitcast.145, f32[8,512,1024]{2,1,0:T(8,128)S(1)} %bitcast.123, f32[8,512]{1,0:T(8,128)S(1)} %copy-done.42, pred[512,1024]{1,0:T(8,128)(4,1)S(1)} %copy-done.10, f32[512,8,64]{0,2,1:T(8,128)} %convolution_bitcast_fusion), kind=kOutput, calls=%fused_computation.154 | convolution fusion | flops 555220480 | bytes 19940352 | tf_op jit(solution)/shard_map/hqk,qhd->khd/dot_general | solution.py:113
  361.8 7.3 %convolution_convert_fusion = bf16[1024,1536]{1,0:T(8,128)(2,1)} fusion(bf16[1024,512]{0,1:T(8,128)(2,1)} %bitcast.166, bf16[1024,512]{0,1:T(8,128)(2,1)S(1)} %bitcast.138, bf16[1024,512]{0,1:T(8,128)(2,1)} %bitcast.141, f32[1024]{0:T(1024)S(1)} %copy-done.50, f32[1024]{0:T(1024)S(1)} %copy-done.39, f32[1024]{0:T(1024)S(1)} %add_rsqrt_fusion.1, ...), kind=kOutput, calls=%fused_computation.39 | convolution fusion | flops 3241672704 | bytes 8404992 | tf_op jit(solution)/shard_map/td,tc->dc/dot_general | solution.py:327
  369.1 12.0 %collective-permute-done.7 = bf16[512,1024]{1,0:T(8,128)(2,1)} collective-permute-done((bf16[512,1024]{1,0:T(8,128)(2,1)}, bf16[512,1024]{1,0:T(8,128)(2,1)}, u32[]{:S(2)}, u32[]{:S(2)}) %collective-permute-start.7) | collective-permute-done | bytes 1048608 | tf_op jit(solution)/shard_map/ppermute | solution.py:127
  387.4 4.1 fusion.13
  391.5 9.4 %fusion.46 = f32[1024,1024]{1,0:T(8,128)S(1)} fusion(bf16[1024,2048]{1,0:T(8,128)(2,1)} %all-gather.11.cloned.1.call-done, f32[1024,2048]{1,0:T(8,128)} %fusion.45, f32[2048]{0:T(1024)S(1)} %copy-done.48), kind=kOutput, calls=%fused_computation.146 | convolution fusion | flops 4315938816 | bytes 16785408 | tf_op jit(solution)/shard_map/tf,df->td/dot_general | solution.py:296
  405.5 22.2 %collective-permute-done.3 = bf16[512,1024]{1,0:T(8,128)(2,1)S(1)} collective-permute-done((bf16[512,1024]{1,0:T(8,128)(2,1)}, bf16[512,1024]{1,0:T(8,128)(2,1)S(1)}, u32[]{:S(2)}, u32[]{:S(2)}) %collective-permute-start.3) | collective-permute-done | bytes 1048608 | tf_op jit(solution)/shard_map/ppermute | solution.py:127
  427.7 4.5 add_add_fusion
  439.1 51.8 %reduce-scatter.11.cloned.1.call-done = bf16[64,2048]{1,0:T(8,128)(2,1)} async-done(((bf16[1024,2048]{1,0:T(8,128)(2,1)}), bf16[64,2048]{1,0:T(8,128)(2,1)}) %reduce-scatter.11.cloned.1.call-update) | async-done | bytes 262160 | tf_op jit(solution)/shard_map/reduce_scatter | solution.py:163
  492.7 68.5 %reduce-scatter.5.cloned.1.call-done = bf16[64,1664]{1,0:T(8,128)(2,1)} async-done(((bf16[1024,1664]{1,0:T(8,128)(2,1)}), bf16[64,1664]{1,0:T(8,128)(2,1)}) %reduce-scatter.5.cloned.1.call-update) | async-done | bytes 213008 | tf_op jit(solution)/shard_map/reduce_scatter | solution.py:163
  (272 shorter events, 126.3 us)
Async XLA Ops:
  7.2 57.8 %all-gather.5.cloned.1.call-start = ((), (), s32[]{:S(2)}) async-start(), calls=%async_computation.4 | async-start | bytes 3620864 | tf_op jit(solution)/shard_map/all_gather | solution.py:159
  15.5 94.1 %all-gather.7.cloned.1.call-start = ((), (), s32[]{:S(2)}) async-start(), calls=%async_computation.5 | async-start | bytes 1114112 | tf_op jit(solution)/shard_map/all_gather | solution.py:159
  16.2 153.6 %all-gather.9.cloned.1.call-start = ((), (), s32[]{:S(2)}) async-start(), calls=%async_computation.6 | async-start | bytes 4456448 | tf_op jit(solution)/shard_map/all_gather | solution.py:159
  17.0 189.0 %all-gather.11.cloned.1.call-start = ((), (), s32[]{:S(2)}) async-start(), calls=%async_computation.7 | async-start | bytes 4456448 | tf_op jit(solution)/shard_map/all_gather | solution.py:159
  17.0 27.3 %collective-permute-start = (bf16[512,1024]{1,0:T(8,128)(2,1)}, bf16[512,1024]{1,0:T(8,128)(2,1)S(1)}, u32[]{:S(2)}, u32[]{:S(2)}) collective-permute-start(bf16[512,1024]{1,0:T(8,128)(2,1)} %param.15), channel_id=1, source_target_pairs={{0,1},{1,0},{2,3},{3,2},{4,5},{5,4},{6,7},{7,6},{8,9},{9,8},{10,11... | collective-permute-start | bytes 3145736 | tf_op jit(solution)/shard_map/ppermute | solution.py:127
  20.1 110.8 %collective-permute-start.4 = (bf16[512,1024]{1,0:T(8,128)(2,1)}, bf16[512,1024]{1,0:T(8,128)(2,1)}, u32[]{:S(2)}, u32[]{:S(2)}) collective-permute-start(bf16[512,1024]{1,0:T(8,128)(2,1)} %param.16), channel_id=1, source_target_pairs={{0,1},{1,0},{2,3},{3,2},{4,5},{5,4},{6,7},{7,6},{8,9},{9,8},{10,11... | collective-permute-start | bytes 3145736 | tf_op jit(solution)/shard_map/ppermute | solution.py:127
  20.2 415.6 %reduce-scatter.7.cloned.1.call-start = ((), (), s32[]{:S(2)}) async-start(), calls=%async_computation.9 | async-start | bytes 1114112 | tf_op jit(solution)/shard_map/reduce_scatter | solution.py:163
  113.4 26.3 %collective-permute-start.2 = (bf16[512,1024]{1,0:T(8,128)(2,1)}, bf16[512,1024]{1,0:T(8,128)(2,1)}, u32[]{:S(2)}, u32[]{:S(2)}) collective-permute-start(bf16[512,1024]{1,0:T(8,128)(2,1)} %get-tuple-element.133), channel_id=1, source_target_pairs={{0,1},{1,0},{2,3},{3,2},{4,5},{5,4},{6,7},{7,6},{8,9},{9,8},{10,11... | collective-permute-start | bytes 3145736 | tf_op jit(solution)/shard_map/ppermute | solution.py:127
  130.3 31.2 %collective-permute-start.1 = (bf16[512,1024]{1,0:T(8,128)(2,1)}, bf16[512,1024]{1,0:T(8,128)(2,1)}, u32[]{:S(2)}, u32[]{:S(2)}) collective-permute-start(bf16[512,1024]{1,0:T(8,128)(2,1)} %get-tuple-element.137), channel_id=1, source_target_pairs={{0,1},{1,0},{2,3},{3,2},{4,5},{5,4},{6,7},{7,6},{8,9},{9,8},{10,11... | collective-permute-start | bytes 3145736 | tf_op jit(solution)/shard_map/ppermute | solution.py:127
  135.2 70.8 %copy-start.47 = (f32[2048]{0:T(1024)}, f32[2048]{0:T(1024)S(1)}, u32[]{:S(2)}) copy-start(f32[2048]{0:T(1024)S(1)} %add.216) | copy-start | bytes 24580
  135.2 26.3 %copy-start.7 = (f32[512,1024]{1,0:T(8,128)S(1)}, f32[512,1024]{1,0:T(8,128)}, u32[]{:S(2)}) copy-start(f32[512,1024]{1,0:T(8,128)} %get-tuple-element.138) | copy-start | bytes 6291460
  206.0 15.1 %copy-start.52 = (bf16[1024,2048]{1,0:T(8,128)(2,1)S(1)}, bf16[1024,2048]{1,0:T(8,128)(2,1)}, u32[]{:S(2)}) copy-start(bf16[1024,2048]{1,0:T(8,128)(2,1)} %all-gather.9.cloned.1.call-done) | copy-start | bytes 12582916
  223.5 26.1 %collective-permute-start.6 = (bf16[512,1024]{1,0:T(8,128)(2,1)S(1)}, bf16[512,1024]{1,0:T(8,128)(2,1)S(1)}, u32[]{:S(2)}, u32[]{:S(2)}) collective-permute-start(bf16[512,1024]{1,0:T(8,128)(2,1)S(1)} %get-tuple-element.140), channel_id=1, source_target_pairs={{0,1},{1,0},{2,3},{3,2},{4,5},{5,4},{6,7},{7,6},{8,9},{9,8},{10,11... | collective-permute-start | bytes 3145736 | tf_op jit(solution)/shard_map/ppermute | solution.py:127
  227.4 43.9 %collective-permute-start.5 = (bf16[512,1024]{1,0:T(8,128)(2,1)S(1)}, bf16[512,1024]{1,0:T(8,128)(2,1)S(1)}, u32[]{:S(2)}, u32[]{:S(2)}) collective-permute-start(bf16[512,1024]{1,0:T(8,128)(2,1)S(1)} %get-tuple-element.142), channel_id=1, source_target_pairs={{0,1},{1,0},{2,3},{3,2},{4,5},{5,4},{6,7},{7,6},{8,9},{9,8},{10,11... | collective-permute-start | bytes 3145736 | tf_op jit(solution)/shard_map/ppermute | solution.py:127
  249.6 22.3 %copy-start.1 = (f32[1024,1024]{1,0:T(8,128)S(1)}, f32[1024,1024]{1,0:T(8,128)}, u32[]{:S(2)}) copy-start(f32[1024,1024]{1,0:T(8,128)} %copy-done) | copy-start | bytes 12582916
  283.2 154.0 %reduce-scatter.9.cloned.1.call-start = ((), (), s32[]{:S(2)}) async-start(), calls=%async_computation.10 | async-start | bytes 4456448 | tf_op jit(solution)/shard_map/reduce_scatter | solution.py:163
  294.1 196.8 %reduce-scatter.11.cloned.1.call-start = ((), (), s32[]{:S(2)}) async-start(), calls=%async_computation.11 | async-start | bytes 4456448 | tf_op jit(solution)/shard_map/reduce_scatter | solution.py:163
  306.9 254.3 %reduce-scatter.5.cloned.1.call-start = ((), (), s32[]{:S(2)}) async-start(), calls=%async_computation.8 | async-start | bytes 3620864 | tf_op jit(solution)/shard_map/reduce_scatter | solution.py:163
  333.4 10.2 %slice-start = ((s8[16777216]{0:T(1024)(128)(4,1)}), s8[4194304]{0:T(1024)(128)(4,1)S(1)}, s32[]{:S(2)}) async-start(s8[16777216]{0:T(1024)(128)(4,1)} %bitcast.122), calls=%async_computation.12 | async-start | bytes 8388608
  349.9 11.9 %copy-start.39 = (f32[1024]{0:T(1024)S(1)}, f32[1024]{0:T(1024)}, u32[]{:S(2)}) copy-start(f32[1024]{0:T(1024)} %copy-done.38) | copy-start | bytes 12292
  350.0 11.8 %copy-start.50 = (f32[1024]{0:T(1024)S(1)}, f32[1024]{0:T(1024)}, u32[]{:S(2)}) copy-start(f32[1024]{0:T(1024)} %copy-done.49) | copy-start | bytes 12292
  356.5 24.6 %collective-permute-start.7 = (bf16[512,1024]{1,0:T(8,128)(2,1)}, bf16[512,1024]{1,0:T(8,128)(2,1)}, u32[]{:S(2)}, u32[]{:S(2)}) collective-permute-start(bf16[512,1024]{1,0:T(8,128)(2,1)} %dynamic-slice_convert_fusion), channel_id=1, source_target_pairs={{0,1},{1,0},{2,3},{3,2},{4,5},{5,4},{6,7},{7,6},{8,9},{9,8},{10,11... | collective-permute-start | bytes 3145736 | tf_op jit(solution)/shard_map/ppermute | solution.py:127
  361.8 19.4 %copy-start.5 = (f32[1024,1024]{1,0:T(8,128)S(1)}, f32[1024,1024]{1,0:T(8,128)}, u32[]{:S(2)}) copy-start(f32[1024,1024]{1,0:T(8,128)} %get-tuple-element.106) | copy-start | bytes 12582916
  361.8 19.4 %copy-start.18 = (f32[1024,1024]{1,0:T(8,128)S(1)}, f32[1024,1024]{1,0:T(8,128)}, u32[]{:S(2)}) copy-start(f32[1024,1024]{1,0:T(8,128)} %copy-done.17) | copy-start | bytes 12582916
  369.1 16.0 %copy-start.27 = (bf16[1024,1]{1,0:T(8,128)(2,1)S(1)}, bf16[1024,1]{1,0:T(8,128)(2,1)}, u32[]{:S(2)}) copy-start(bf16[1024,1]{1,0:T(8,128)(2,1)} %stack.63) | copy-start | bytes 6148
  369.1 16.0 %copy-start.28 = (bf16[1024,1]{1,0:T(8,128)(2,1)S(1)}, bf16[1024,1]{1,0:T(8,128)(2,1)}, u32[]{:S(2)}) copy-start(bf16[1024,1]{1,0:T(8,128)(2,1)} %stack.62) | copy-start | bytes 6148
  369.1 16.0 %copy-start.29 = (bf16[1024,1]{1,0:T(8,128)(2,1)S(1)}, bf16[1024,1]{1,0:T(8,128)(2,1)}, u32[]{:S(2)}) copy-start(bf16[1024,1]{1,0:T(8,128)(2,1)} %reduce_sum.236) | copy-start | bytes 6148
  369.1 16.0 %copy-start.30 = (bf16[1024,3]{1,0:T(8,128)(2,1)S(1)}, bf16[1024,3]{1,0:T(8,128)(2,1)}, u32[]{:S(2)}) copy-start(bf16[1024,3]{1,0:T(8,128)(2,1)} %reshape.290) | copy-start | bytes 18436
  391.5 36.2 %copy-start.40 = (f32[1024]{0:T(1024)S(1)}, f32[1024]{0:T(1024)}, u32[]{:S(2)}) copy-start(f32[1024]{0:T(1024)} %get-tuple-element.77) | copy-start | bytes 12292
  404.0 23.8 %collective-permute-start.3 = (bf16[512,1024]{1,0:T(8,128)(2,1)}, bf16[512,1024]{1,0:T(8,128)(2,1)S(1)}, u32[]{:S(2)}, u32[]{:S(2)}) collective-permute-start(bf16[512,1024]{1,0:T(8,128)(2,1)} %dynamic-slice_convert_fusion.1), channel_id=1, source_target_pairs={{0,1},{1,0},{2,3},{3,2},{4,5},{5,4},{6,7},{7,6},{8,9},{9,8},{10,11... | collective-permute-start | bytes 3145736 | tf_op jit(solution)/shard_map/ppermute | solution.py:127
  405.5 26.8 %copy-start.6 = (f32[1024,1024]{1,0:T(8,128)S(1)}, f32[1024,1024]{1,0:T(8,128)}, u32[]{:S(2)}) copy-start(f32[1024,1024]{1,0:T(8,128)} %get-tuple-element.106) | copy-start | bytes 12582916
  562.9 6.7 %collective-permute-start.8 = (f32[64,2]{1,0:T(8,128)S(1)}, f32[64,2]{1,0:T(8,128)S(1)}, u32[]{:S(2)}, u32[]{:S(2)}) collective-permute-start(f32[64,2]{1,0:T(8,128)S(1)} %slice.207), channel_id=1, source_target_pairs={{0,1},{1,0},{2,3},{3,2},{4,5},{5,4},{6,7},{7,6},{8,9},{9,8},{10,11... | collective-permute-start | bytes 1544 | tf_op jit(solution)/shard_map/ppermute | solution.py:127
  (44 other events, 203.3 us)
Sparse Core Ops, SparseCore 0:
  15.6 49.2 all-gather.4
  67.1 36.3 all-gather.6
  105.7 49.3 all-gather.8
  157.1 48.9 all-gather.10
  283.3 56.1 reduce-scatter.6
  343.3 71.8 reduce-scatter.8
  419.1 71.7 reduce-scatter.10
  494.7 66.4 reduce-scatter.4
